TPU v7x, 256 devices: a whole 4x4x8 slice. The times are simulated.
256 devices in a mesh: slab: 16 (over x_hi, y, core), batch: 16 (over x_lo, z).
Axes of the slice: x: 4 (x_hi: 2, x_lo: 2; x = x_hi * 2 + x_lo), y: 4, z: 8, core: 2. Of those that a mesh axis runs over, the one named last changes fastest.
Arguments:
- volumes: bfloat16 [256, 2, 16384], P('slab', None, 'batch'), may hold values from -6 to 6
- band_weights: bfloat16 [2, 1024, 32], P(None, 'slab'), may hold values from -1 to 1
- band_start: int32 [2, 1024], P(None, 'slab'), may hold values from 0 to 224
- images: bfloat16 [6144, 16384], P('batch'), may hold values from -7 to 7
- noise_precision: float32 [6144], P('batch'), may hold values from 0.005004883 to 0.050048828
- log_prior: float32 [2, 1024], P(None, 'slab'), may hold values from -4 to 4
Outputs:
- responsibilities: float32 [2, 1024, 6144], P(None, 'slab', 'batch')
- log_evidence: float32 [6144], P('batch')
- backprojection: float32 [256, 2, 16384], P('slab', None, 'batch')
All inputs are finite; a program needn't handle non-finite values.
Results may differ from a plain program's by a relative error of at most 0.0069.
Values may be sent and summed in bfloat16 or wider, within the bound.
A program may use at most 64 MiB of HBM per device.

v0:
```python
import jax
import jax.numpy as jnp
from jax import lax
from jax.sharding import PartitionSpec as P


def joined_along(pieces, dim):
    pieces = jnp.moveaxis(pieces, 0, dim)
    shape = pieces.shape
    return pieces.reshape(*shape[:dim], shape[dim] * shape[dim + 1], *shape[dim + 2 :])


def copy_for_each(x, axis):
    copies = jnp.broadcast_to(x, (lax.axis_size(axis), *x.shape))
    return lax.all_to_all(copies, axis, split_axis=0, concat_axis=0, tiled=True)


def collect(x, axis, dim):
    return joined_along(copy_for_each(x, axis), dim)


def gathered_once(x, axis):
    leaves = jax.tree.leaves(x)
    sequence = sorted(range(len(leaves)), key=lambda k: -leaves[k].size)
    width = (1, *leaves[sequence[0]].shape)[-1]
    lines = [
        jnp.pad(leaves[k].reshape(-1), (0, -leaves[k].size % width)).reshape(-1, width)
        for k in sequence
    ]
    both, at, found = (copy_for_each(jnp.concatenate(lines), axis), 0, {})
    for k, line in zip(sequence, lines):
        piece = both[:, at : at + len(line)].reshape(len(both), -1)
        found[k] = piece[:, : leaves[k].size].reshape(-1, *leaves[k].shape)
        at += len(line)
    numbers = iter(range(len(leaves)))
    return jax.tree.map(lambda _: found[next(numbers)], x)


def folded_in_pairs(pieces, combine):
    while len(jax.tree.leaves(pieces)[0]) > 1:
        pieces = jax.vmap(combine)(
            *(jax.tree.map(lambda part: part[side::2], pieces) for side in (0, 1))
        )
    return jax.tree.map(lambda part: part[0], pieces)


def joined_all(x, axis, combine):
    pieces = gathered_once(x, axis)
    return folded_in_pairs(pieces, combine)


def cut_along(x, dim, count):
    before, after = (x.shape[:dim], x.shape[dim + 1 :])
    return jnp.moveaxis(x.reshape(*before, count, -1, *after), dim, 0)


def sum_at_owner(x, axis, dim):
    pieces = cut_along(x, dim, lax.axis_size(axis))
    arrived = lax.all_to_all(pieces, axis, split_axis=0, concat_axis=0, tiled=True)
    return arrived.sum(axis=0)


def build_slice(band_weights, band_start, planes):
    offsets = planes[None, None, :] - band_start[:, :, None]
    taps = jnp.arange(band_weights.shape[2], dtype=jnp.int32)
    hits = offsets[..., None] == taps
    values = jnp.where(hits, band_weights.astype(jnp.float32)[:, :, None, :], jnp.float32(0.0))
    return jnp.sum(values, axis=-1)


def combine_scores(first, second):
    top_one, total_one = first
    top_two, total_two = second
    joined = jnp.maximum(top_one, top_two)
    return (joined, total_one * jnp.exp(top_one - joined) + total_two * jnp.exp(top_two - joined))


def local(volumes, band_weights, band_start, images, noise_precision, log_prior):
    plane_count, classes, block = volumes.shape
    all_planes = plane_count * lax.axis_size("slab")
    slice_own = build_slice(band_weights, band_start, jnp.arange(all_planes, dtype=jnp.int32))
    gathered = collect(volumes, "slab", 0)
    projection = jnp.einsum(
        "koz,zkp->okp", slice_own.astype(jnp.bfloat16), gathered, preferred_element_type=jnp.float32
    ).astype(jnp.bfloat16)
    piece = lax.all_gather(projection, "batch", axis=2, tiled=True)
    columns = images
    inner = jnp.einsum("okp,np->kon", piece, columns, preferred_element_type=jnp.float32)
    wide = piece.astype(jnp.float32)
    inner, energy = (inner, jnp.sum(wide * wide, axis=2))
    score = (
        noise_precision[None, None, :] * (inner - 0.5 * energy.T[:, :, None])
        + log_prior[:, :, None]
    )
    local_top = jnp.max(score, axis=(0, 1))
    local_total = jnp.sum(jnp.exp(score - local_top[None, None, :]), axis=(0, 1))
    top, total = joined_all((local_top, local_total), "slab", combine_scores)
    log_evidence = top + jnp.log(total)
    responsibilities = jnp.exp(score - log_evidence[None, None, :])
    weights = responsibilities.astype(jnp.bfloat16)
    columns = images
    image_sum = lax.psum_scatter(
        jnp.einsum("np,kon->pko", columns, weights, preferred_element_type=jnp.float32),
        "batch",
        scatter_dimension=0,
        tiled=True,
    )
    backprojection = sum_at_owner(
        jnp.einsum("koz,pko->zkp", slice_own, image_sum, precision=lax.Precision.HIGHEST), "slab", 0
    )
    return (responsibilities, log_evidence, backprojection)


def solution(mesh):
    in_specs = (
        P("slab", None, "batch"),
        P(None, "slab", None),
        P(None, "slab"),
        P("batch", None),
        P("batch"),
        P(None, "slab"),
    )
    out_specs = (P(None, "slab", "batch"), P("batch"), P("slab", None, "batch"))
    return jax.shard_map(local, mesh=mesh, in_specs=in_specs, out_specs=out_specs, check_vma=False)
```

profile of v0, /device:TPU:1, one launch (start us, length us, event | category | flops | bytes accessed | tf_op | source)
XLA Modules:
  0.0 288.5 jit_solution(14780554154317257893)
XLA Ops:
  7.2 0.9 copy.20
  8.0 1.1 broadcast_in_dim.18
  9.1 8.4 %all-to-all-start = ((bf16[16,16,2,1024]{3,1,2,0:T(8,128)(2,1)}), bf16[16,16,2,1024]{3,1,2,0:T(8,128)(2,1)S(1)}, u32[]{:S(2)}, u32[]{:S(2)}) async-start(bf16[16,16,2,1024]{3,1,2,0:T(8,128)(2,1)} %broadcast_in_dim.18), calls=%async_computation | async-start | bytes 2097152 | tf_op jit(solution)/shard_map/all_to_all | solution.py:15
  17.6 0.0 all-gather.2.cloned.1.call-start
  17.6 0.8 copy.19
  18.4 0.8 iota_subtract_fusion
  19.2 0.0 copy-start.3
  19.2 0.0 copy-start.4
  19.2 1.1 select_reduce_fusion
  20.3 14.3 %all-to-all-done = bf16[16,16,2,1024]{3,1,2,0:T(8,128)(2,1)S(1)} async-done(((bf16[16,16,2,1024]{3,1,2,0:T(8,128)(2,1)}), bf16[16,16,2,1024]{3,1,2,0:T(8,128)(2,1)S(1)}, u32[]{:S(2)}, u32[]{:S(2)}) %all-to-all-start) | async-done | bytes 1048608 | tf_op jit(solution)/shard_map/all_to_all | solution.py:15
  34.7 0.1 copy.21
  34.8 1.0 fusion.3
  35.8 0.0 all-gather.2.cloned.1.call-update
  35.8 0.0 reduce-scatter.2.cloned.1.call-start
  35.8 65.5 %all-gather.2.cloned.1.call-done = bf16[64,2,16384]{2,0,1:T(8,128)(2,1)} async-done(((bf16[64,2,1024]{2,0,1:T(8,128)(2,1)}), bf16[64,2,16384]{2,0,1:T(8,128)(2,1)}) %all-gather.2.cloned.1.call-update) | async-done | bytes 4194320 | tf_op jit(solution)/shard_map/all_gather | solution.py:86
  101.4 3.3 %multiply_reduce_fusion = f32[64,2]{0,1:T(2,128)S(1)} fusion(bf16[64,2,16384]{2,0,1:T(8,128)(2,1)} %all-gather.2.cloned.1.call-done), kind=kLoop, calls=%fused_computation.4 | loop fusion | flops 6291328 | bytes 4194816 | tf_op jit(solution)/shard_map/reduce_sum | solution.py:90
  104.7 0.0 copy-done.3
  104.7 0.0 copy-done.4
  104.7 0.1 copy-done
  104.8 8.4 %fusion.21 = (f32[384]{0:T(512)S(1)}, f32[2,64,384]{2,1,0:T(8,128)S(1)}) fusion(f32[2,64]{1,0:T(2,128)S(1)} %copy-done.4, f32[2,64]{1,0:T(2,128)S(1)} %multiply_bitcast_fusion, bf16[64,2,16384]{2,0,1:T(8,128)(2,1)S(1)} %copy-done, bf16[384,16384]{1,0:T(8,128)(2,1)} %param.9, f32[384]{0:T(512)S(1)} %copy-done.3), kind=kOutput, calls=%fused_computation.32 | convolution fusion | flops 1610808960 | bytes 16977920 | tf_op jit(solution)/shard_map/okp,np->kon/dot_general | solution.py:88
  113.2 0.1 exponential_reduce_fusion
  113.3 24.0 %all_to_all.15 = f32[16,2,384]{2,1,0:T(2,128)S(1)} all-to-all(f32[16,2,384]{2,1,0:T(2,128)S(1)} %broadcast_in_dim.19), channel_id=1, replica_groups=mesh['slab'=16,'batch'=16] {'slab'}, dimensions={0} | all-to-all | bytes 98304 | tf_op jit(solution)/shard_map/all_to_all | solution.py:15
  137.7 0.0 copy-start.2
  137.8 0.0 copy-start.1
  137.8 10.2 %convolution_bitcast_fusion = f32[16384,2,64]{0,2,1:T(8,128)} fusion(bf16[384,16384]{1,0:T(8,128)(2,1)} %param.9, f32[2,64,384]{2,1,0:T(8,128)S(1)} %subtract_exponential_fusion), kind=kOutput, calls=%fused_computation | convolution fusion | flops 1610661888 | bytes 21168128 | tf_op jit(solution)/shard_map/np,kon->pko/dot_general | solution.py:103
  148.0 0.0 reduce-scatter.2.cloned.1.call-update
  148.0 94.6 %reduce-scatter.2.cloned.1.call-done = f32[1024,2,64]{0,2,1:T(8,128)} async-done(((f32[16384,2,64]{0,2,1:T(8,128)}), f32[1024,2,64]{0,2,1:T(8,128)}) %reduce-scatter.2.cloned.1.call-update) | async-done | bytes 524304 | tf_op jit(solution)/shard_map/reduce_scatter | solution.py:102
  242.7 2.9 fusion.22
  245.5 0.2 copy.23
  245.8 35.0 %all_to_all.16 = f32[16,16,2,1024]{3,1,2,0:T(8,128)S(1)} all-to-all(f32[16,16,2,1024]{3,1,2,0:T(8,128)S(1)} %copy.23), channel_id=1, replica_groups=mesh['slab'=16,'batch'=16] {'slab'}, dimensions={0} | all-to-all | bytes 4194304 | tf_op jit(solution)/shard_map/all_to_all | solution.py:59
  280.7 0.1 reduce_sum.39
  280.9 0.8 copy.25
  (27 shorter events, 0.5 us)
Async XLA Ops:
  9.1 25.5 %all-to-all-start = ((bf16[16,16,2,1024]{3,1,2,0:T(8,128)(2,1)}), bf16[16,16,2,1024]{3,1,2,0:T(8,128)(2,1)S(1)}, u32[]{:S(2)}, u32[]{:S(2)}) async-start(bf16[16,16,2,1024]{3,1,2,0:T(8,128)(2,1)} %broadcast_in_dim.18), calls=%async_computation | async-start | bytes 2097152 | tf_op jit(solution)/shard_map/all_to_all | solution.py:15
  17.6 83.8 %all-gather.2.cloned.1.call-start = ((), (), s32[]{:S(2)}) async-start(), calls=%async_computation.4 | async-start | bytes 4456448 | tf_op jit(solution)/shard_map/all_gather | solution.py:86
  19.2 85.5 %copy-start.3 = (f32[384]{0:T(512)S(1)}, f32[384]{0:T(512)}, u32[]{:S(2)}) copy-start(f32[384]{0:T(512)} %param.10) | copy-start | bytes 4612
  19.2 85.5 %copy-start.4 = (f32[2,64]{1,0:T(2,128)S(1)}, f32[2,64]{1,0:T(2,128)}, u32[]{:S(2)}) copy-start(f32[2,64]{1,0:T(2,128)} %param.11) | copy-start | bytes 1540
  35.8 206.9 %reduce-scatter.2.cloned.1.call-start = ((), (), s32[]{:S(2)}) async-start(), calls=%async_computation.5 | async-start | bytes 8912896 | tf_op jit(solution)/shard_map/reduce_scatter | solution.py:102
  101.4 3.4 %copy-start = (bf16[64,2,16384]{2,0,1:T(8,128)(2,1)S(1)}, bf16[64,2,16384]{2,0,1:T(8,128)(2,1)}, u32[]{:S(2)}) copy-start(bf16[64,2,16384]{2,0,1:T(8,128)(2,1)} %all-gather.2.cloned.1.call-done) | copy-start | bytes 12582916
  137.7 10.3 %copy-start.2 = (f32[384]{0:T(512)}, f32[384]{0:T(512)S(1)}, u32[]{:S(2)}) copy-start(f32[384]{0:T(512)S(1)} %add_reduce_fusion) | copy-start | bytes 4612
  137.8 10.2 %copy-start.1 = (f32[2,64,384]{2,1,0:T(8,128)}, f32[2,64,384]{2,1,0:T(8,128)S(1)}, u32[]{:S(2)}) copy-start(f32[2,64,384]{2,1,0:T(8,128)S(1)} %subtract_exponential_fusion) | copy-start | bytes 589828
Sparse Core Ops, SparseCore 0:
  35.9 65.4 all-gather.1
  148.1 94.4 reduce-scatter.1
where the time goes:
time: 289 us; the launch traced here: 288 us
  waiting for transfers between devices  175 us (61%)
  blocking collectives  58.9 us (20%)
  matrix products  22.5 us (8%)
  between operations  14.2 us (5%)
  starting transfers between devices  8.51 us (3%)
  other arithmetic  5.44 us (2%)
  local copies, waits for them, and re-layouts  4.35 us (2%)
    reduce_scatter x1, waiting for transfers between devices, local(): lax.psum_scatter(jnp.einsum('np,kon->pko', columns, weights, preferred_el...  94.6 us
    all_gather x1, waiting for transfers between devices, local(): piece = lax.all_gather(projection, 'batch', axis=2, tiled=True)  65.5 us
    all_to_all x1, blocking collectives, sum_at_owner(): lax.all_to_all(pieces, axis, split_axis=0, concat_axis=0, tiled=True)  35 us
    all_to_all x1, blocking collectives, copy_for_each(): return lax.all_to_all(copies, axis, split_axis=0, concat_axis=0, tiled=True)  24 us
    all_to_all x1, waiting for transfers between devices, copy_for_each(): return lax.all_to_all(copies, axis, split_axis=0, concat_axis=0, tiled=True)  14.3 us
    dot_general x1, matrix products, local(): jnp.einsum('np,kon->pko', columns, weights, preferred_element_type=jnp.fl...  10.2 us
    all_to_all x1, starting transfers between devices, copy_for_each(): return lax.all_to_all(copies, axis, split_axis=0, concat_axis=0, tiled=True)  8.44 us
    dot_general x1, matrix products, local(): jnp.einsum('okp,np->kon', piece, columns, preferred_element_type=jnp.floa...  8.39 us
  transfers between devices with their start and end apart: 3, of which 3 were waited for; matrix products, arithmetic and copies ran while one was open for 1% of the time, Pallas kernels for 0%

commit v1 on v0

--- a/solution.py
+++ b/solution.py
@@ -83,7 +83,9 @@
     projection = jnp.einsum(
         "koz,zkp->okp", slice_own.astype(jnp.bfloat16), gathered, preferred_element_type=jnp.float32
     ).astype(jnp.bfloat16)
-    piece = lax.all_gather(projection, "batch", axis=2, tiled=True)
+    piece = jnp.concatenate(
+        lax.all_to_all(jnp.stack([projection] * lax.axis_size("batch")), "batch", 0, 0), axis=2
+    )
     columns = images
     inner = jnp.einsum("okp,np->kon", piece, columns, preferred_element_type=jnp.float32)
     wide = piece.astype(jnp.float32)

time: 289 us -> 312 us (1.080)
  blocking collectives: 58.9 us -> 150 us
  waiting for transfers between devices: 175 us -> 110 us
    all_to_all x0 -> x1, blocking collectives: none -> 99.9 us  [local(): lax.all_to_all(jnp.stack([projection] * lax.axis_size('batch')), 'batch',...]
    all_gather x1 -> x0, waiting for transfers between devices: 65.5 us -> none  [local(): piece = lax.all_gather(projection, 'batch', axis=2, tiled=True)]
    all_to_all x1, blocking collectives: 24 us -> 14.7 us  [copy_for_each(): return lax.all_to_all(copies, axis, split_axis=0, concat_axis=0, tiled=True)]
  transfers between devices with their start and end apart: 3 -> 2, of which waited for: 3 -> 2; matrix products, arithmetic and copies ran while one was open for 1% -> 1% of each run, Pallas kernels for 0% -> 0%
where the time goes in v1:
time: 312 us
  blocking collectives  150 us (48%)
  waiting for transfers between devices  110 us (35%)
  matrix products  19.4 us (6%)
  between operations  14.2 us (5%)
  starting transfers between devices  8.47 us (3%)
  local copies, waits for them, and re-layouts  7.14 us (2%)
    all_to_all x1, blocking collectives, local(): lax.all_to_all(jnp.stack([projection] * lax.axis_size('batch')), 'batch',...  99.9 us
    reduce_scatter x1, waiting for transfers between devices, local(): lax.psum_scatter(jnp.einsum('np,kon->pko', columns, weights, preferred_el...  95.4 us
    all_to_all x1, blocking collectives, sum_at_owner(): lax.all_to_all(pieces, axis, split_axis=0, concat_axis=0, tiled=True)  35 us
    all_to_all x1, blocking collectives, copy_for_each(): return lax.all_to_all(copies, axis, split_axis=0, concat_axis=0, tiled=True)  14.7 us
    all_to_all x1, waiting for transfers between devices, copy_for_each(): return lax.all_to_all(copies, axis, split_axis=0, concat_axis=0, tiled=True)  14.4 us
    dot_general x1, matrix products, local(): jnp.einsum('np,kon->pko', columns, weights, preferred_element_type=jnp.fl...  10.2 us
    all_to_all x1, starting transfers between devices, copy_for_each(): return lax.all_to_all(copies, axis, split_axis=0, concat_axis=0, tiled=True)  8.44 us
  transfers between devices with their start and end apart: 2, of which 2 were waited for; matrix products, arithmetic and copies ran while one was open for 1% of the time, Pallas kernels for 0%

profile of v1, /device:TPU:1, one launch (start us, length us, event | category | flops | bytes accessed | tf_op | source)
XLA Modules:
  0.0 311.7 jit_solution(100258624626324401)
XLA Ops:
  7.2 0.9 copy.21
  8.0 1.1 broadcast_in_dim.18
  9.1 8.4 %all-to-all-start = ((bf16[16,16,2,1024]{3,1,2,0:T(8,128)(2,1)}), bf16[16,16,2,1024]{3,1,2,0:T(8,128)(2,1)S(1)}, u32[]{:S(2)}, u32[]{:S(2)}) async-start(bf16[16,16,2,1024]{3,1,2,0:T(8,128)(2,1)} %broadcast_in_dim.18), calls=%async_computation | async-start | bytes 2097152 | tf_op jit(solution)/shard_map/all_to_all | solution.py:15
  17.6 0.0 reduce-scatter.2.cloned.1.call-start
  17.6 0.8 copy.20
  18.4 0.8 iota_subtract_fusion
  19.2 1.1 select_reduce_fusion
  20.3 14.4 %all-to-all-done = bf16[16,16,2,1024]{3,1,2,0:T(8,128)(2,1)S(1)} async-done(((bf16[16,16,2,1024]{3,1,2,0:T(8,128)(2,1)}), bf16[16,16,2,1024]{3,1,2,0:T(8,128)(2,1)S(1)}, u32[]{:S(2)}, u32[]{:S(2)}) %all-to-all-start) | async-done | bytes 1048608 | tf_op jit(solution)/shard_map/all_to_all | solution.py:15
  34.7 0.1 copy.22
  34.8 0.3 fusion.3
  35.1 0.0 slice-start
  35.1 0.5 stack.2
  35.6 0.0 slice-start.1
  35.6 99.9 %all_to_all.20 = bf16[16,64,2,1024]{3,1,2,0:T(8,128)(2,1)S(1)} all-to-all(bf16[16,64,2,1024]{3,1,2,0:T(8,128)(2,1)S(1)} %stack.2), channel_id=1, replica_groups=mesh['slab'=16,'batch'=16] {'batch'}, dimensions={0} | all-to-all | bytes 8388608 | tf_op jit(solution)/shard_map/all_to_all | solution.py:87
  135.5 1.0 multiply_reduce_fusion
  136.5 2.4 copy.31
  138.9 0.0 slice-done
  138.9 0.0 slice-done.1
  138.9 0.0 copy-done.2
  138.9 6.0 %fusion.21 = (f32[384]{0:T(512)S(1)}, f32[2,64,384]{2,1,0:T(8,128)S(1)}) fusion(f32[2,64]{1,0:T(2,128)S(1)} %copy-done.3, f32[2,64]{1,0:T(2,128)S(1)} %multiply_bitcast_fusion, bf16[64,2,16384]{2,0,1:T(8,128)(2,1)} %bitcast.48, bf16[384,16384]{1,0:T(8,128)(2,1)S(1)} %bitcast.46, f32[384]{0:T(512)S(1)} %copy-done.2), kind=kOutput, calls=%fused_computation.32 | convolution fusion | flops 1610808960 | bytes 16977920 | tf_op jit(solution)/shard_map/okp,np->kon/dot_general | solution.py:90
  145.0 0.1 exponential_reduce_fusion
  145.1 14.7 %all_to_all.21 = f32[16,2,384]{2,1,0:T(2,128)S(1)} all-to-all(f32[16,2,384]{2,1,0:T(2,128)S(1)} %broadcast_in_dim.19), channel_id=1, replica_groups=mesh['slab'=16,'batch'=16] {'slab'}, dimensions={0} | all-to-all | bytes 98304 | tf_op jit(solution)/shard_map/all_to_all | solution.py:15
  160.2 0.0 copy-start.1
  160.2 0.0 copy-start
  160.2 10.2 %convolution_bitcast_fusion = f32[16384,2,64]{0,2,1:T(8,128)} fusion(bf16[384,16384]{1,0:T(8,128)(2,1)} %param.9, f32[2,64,384]{2,1,0:T(8,128)S(1)} %subtract_exponential_fusion), kind=kOutput, calls=%fused_computation | convolution fusion | flops 1610661888 | bytes 21168128 | tf_op jit(solution)/shard_map/np,kon->pko/dot_general | solution.py:105
  170.5 0.0 reduce-scatter.2.cloned.1.call-update
  170.5 95.4 %reduce-scatter.2.cloned.1.call-done = f32[1024,2,64]{0,2,1:T(8,128)} async-done(((f32[16384,2,64]{0,2,1:T(8,128)}), f32[1024,2,64]{0,2,1:T(8,128)}) %reduce-scatter.2.cloned.1.call-update) | async-done | bytes 524304 | tf_op jit(solution)/shard_map/reduce_scatter | solution.py:104
  265.9 2.9 fusion.22
  268.8 0.2 copy.25
  269.0 35.0 %all_to_all.22 = f32[16,16,2,1024]{3,1,2,0:T(8,128)S(1)} all-to-all(f32[16,16,2,1024]{3,1,2,0:T(8,128)S(1)} %copy.25), channel_id=1, replica_groups=mesh['slab'=16,'batch'=16] {'slab'}, dimensions={0} | all-to-all | bytes 4194304 | tf_op jit(solution)/shard_map/all_to_all | solution.py:59
  304.0 0.1 reduce_sum.39
  304.1 0.8 copy.27
  (32 shorter events, 0.5 us)
Async XLA Ops:
  9.1 25.5 %all-to-all-start = ((bf16[16,16,2,1024]{3,1,2,0:T(8,128)(2,1)}), bf16[16,16,2,1024]{3,1,2,0:T(8,128)(2,1)S(1)}, u32[]{:S(2)}, u32[]{:S(2)}) async-start(bf16[16,16,2,1024]{3,1,2,0:T(8,128)(2,1)} %broadcast_in_dim.18), calls=%async_computation | async-start | bytes 2097152 | tf_op jit(solution)/shard_map/all_to_all | solution.py:15
  17.6 248.3 %reduce-scatter.2.cloned.1.call-start = ((), (), s32[]{:S(2)}) async-start(), calls=%async_computation.5 | async-start | bytes 8912896 | tf_op jit(solution)/shard_map/reduce_scatter | solution.py:104
  35.1 103.8 %slice-start = ((s8[12582912]{0:T(1024)(128)(4,1)}), s8[4194304]{0:T(1024)(128)(4,1)S(1)}, s32[]{:S(2)}) async-start(s8[12582912]{0:T(1024)(128)(4,1)} %bitcast.45), calls=%async_computation.6 | async-start | bytes 8388608
  35.6 103.3 %slice-start.1 = ((s8[12582912]{0:T(1024)(128)(4,1)}), s8[4194304]{0:T(1024)(128)(4,1)S(1)}, s32[]{:S(2)}) async-start(s8[12582912]{0:T(1024)(128)(4,1)} %bitcast.45), calls=%async_computation.7 | async-start | bytes 8388608
  135.5 3.4 %slice-start.2 = ((s8[12582912]{0:T(1024)(128)(4,1)}), s8[4194304]{0:T(1024)(128)(4,1)S(1)}, s32[]{:S(2)}) async-start(s8[12582912]{0:T(1024)(128)(4,1)} %bitcast.45), calls=%async_computation.8 | async-start | bytes 8388608
  136.5 2.4 copy-start.2
  136.5 2.4 copy-start.3
  160.2 10.3 %copy-start.1 = (f32[384]{0:T(512)}, f32[384]{0:T(512)S(1)}, u32[]{:S(2)}) copy-start(f32[384]{0:T(512)S(1)} %add_reduce_fusion) | copy-start | bytes 4612
  160.2 10.2 %copy-start = (f32[2,64,384]{2,1,0:T(8,128)}, f32[2,64,384]{2,1,0:T(8,128)S(1)}, u32[]{:S(2)}) copy-start(f32[2,64,384]{2,1,0:T(8,128)S(1)} %subtract_exponential_fusion) | copy-start | bytes 589828
Sparse Core Ops, SparseCore 0:
  170.6 95.2 reduce-scatter.1
